TPU v7x, 128 devices: a whole 4x4x4 slice. The times are simulated.
128 devices in a mesh: lat: 8 (over z, core), lon: 16 (over x, y).
Axes of the slice: x: 4, y: 4, z: 4, core: 2. Of those that a mesh axis runs over, the one named last changes fastest.
Arguments:
- surface: float32 [2048, 16384], P('lat', 'lon'), may hold values from -24 to 24
- bathymetry: float32 [2048, 16384], P('lat', 'lon'), may hold values from 0.1 to 1
- land_sea: int32 [2048, 16384], P('lat', 'lon'), may hold values 0 or 1
- flux_lon: float32 [2048, 16384], P('lat', 'lon'), may hold values from -12 to 12
- flux_lat: float32 [2048, 16384], P('lat', 'lon'), may hold values from -12 to 12
Outputs:
- surface_next: float32 [2048, 16384], P('lat', 'lon')
- flux_lon_next: float32 [2048, 16384], P('lat', 'lon')
- flux_lat_next: float32 [2048, 16384], P('lat', 'lon')
All inputs are finite; a program needn't handle non-finite values. No bound on the sum of `land_sea` on one device may be relied on, other than what follows from the above.
Results may differ from a plain program's by a relative error of at most 0.0001.
Values sent between devices are 32-bit elements; how exact they have to be, the bound alone decides.
A program may use at most 64 MiB of HBM per device.

v0:
```python
import jax
import jax.numpy as jnp
from jax import lax
from jax.sharding import PartitionSpec as P

ITERS = 3
courant = -0.4
dispersion = 40.0
continuity = -0.5


def from_behind(value, axis, steps):
    count = lax.axis_size(axis)
    leading, last = (max(0, -steps), min(count, count - steps))
    return lax.ppermute(value, axis, [(source, source + steps) for source in range(leading, last)])


def upper_cells(stacked):
    north_row = from_behind(stacked[:, :1, :], "lat", -1)
    east_col = from_behind(stacked[:, :, :1], "lon", -1)
    eastern = jnp.concatenate([stacked[:, :, 1:], east_col], axis=2)
    northern = jnp.concatenate([stacked[:, 1:, :], north_row], axis=1)
    return (eastern, northern)


def lower_fluxes(field):
    south_row = from_behind(field[:, -1:, :], "lat", 1)
    west_col = from_behind(field[:, :, -1:], "lon", 1)
    western = jnp.concatenate([west_col, field[:, :, :-1]], axis=2)
    southern = jnp.concatenate([south_row, field[:, :-1, :]], axis=1)
    return (western, southern)


def divergence(field):
    western, southern = lower_fluxes(field)
    return field[0] - western[0] + field[1] - southern[1]


def gradient_back(field):
    diverge = divergence(field)
    eastern, northern = upper_cells(diverge[None])
    return jnp.stack([diverge - eastern[0], diverge - northern[0]])


def operate(field, wet, inverse):
    return wet * (inverse * field + gradient_back(field))


def sums(*pairs):
    local = jnp.stack([jnp.sum(x * y) for x, y in pairs])
    return lax.psum(local, ("lat", "lon"))


def per_device(surface, bathymetry, land_sea, flux_lon, flux_lat):
    sea = land_sea.astype(jnp.float32)
    cells = jnp.stack([surface, bathymetry, sea])
    eastern, northern = upper_cells(cells)
    wet = jnp.stack([sea * eastern[2], sea * northern[2]])
    depth = jnp.stack([0.5 * (bathymetry + eastern[1]), 0.5 * (bathymetry + northern[1])])
    slope = jnp.stack([eastern[0] - surface, northern[0] - surface])
    start = wet * (jnp.stack([flux_lon, flux_lat]) - courant * depth * slope)
    inverse = 1.0 / (dispersion * depth * depth)
    right_side = wet * inverse * start
    solution = start
    residual = right_side - operate(start, wet, inverse)
    applied = operate(residual, wet, inverse)
    norm_now, curve = sums((residual, residual), (residual, applied))
    direction, image = (residual, applied)
    for step in range(ITERS):
        alpha = norm_now / curve
        solution = solution + alpha * direction
        if step == ITERS - 1:
            break
        residual = residual - alpha * image
        applied = operate(residual, wet, inverse)
        norm_next, r_ar, r_ap = sums((residual, residual), (residual, applied), (residual, image))
        beta = norm_next / norm_now
        curve = r_ar + 2.0 * beta * r_ap + beta * beta * curve
        direction = residual + beta * direction
        image = applied + beta * image
        norm_now = norm_next
    surface_next = surface - continuity * divergence(solution)
    return (surface_next, solution[0], solution[1])


def solution(mesh):
    in_specs = (P("lat", "lon"), P("lat", "lon"), P("lat", "lon"), P("lat", "lon"), P("lat", "lon"))
    out_specs = (P("lat", "lon"), P("lat", "lon"), P("lat", "lon"))
    return jax.shard_map(
        per_device, mesh=mesh, in_specs=in_specs, out_specs=out_specs, check_vma=False
    )
```

profile of v0, /device:TPU:3, one launch (start us, length us, event | category | flops | bytes accessed | tf_op | source)
XLA Modules:
  0.0 372.1 jit_solution(16811035652455948281)
XLA Ops:
  0.7 1.5 convert_bitcast_fusion
  2.5 2.6 collective-permute-start.1
  5.1 4.6 %collective-permute-start = (f32[3,256,1]{2,1,0:T(8,128)S(1)}, f32[3,256,1]{2,1,0:T(8,128)S(1)}, u32[]{:S(2)}, u32[]{:S(2)}) collective-permute-start(f32[3,256,1]{2,1,0:T(8,128)S(1)} %pad_maximum_fusion.15), channel_id=1, source_target_pairs={{1,0},{2,1},{3,2},{4,3},{5,4},{6,5},{7,6},{8,7},{9,8},{10,9},{11,1... | collective-permute-start | bytes 9224 | tf_op jit(solution)/shard_map/ppermute | solution.py:15
  10.0 0.4 slice.269
  10.4 0.9 slice.266
  11.3 7.3 %collective-permute-done = f32[3,256,1]{2,1,0:T(8,128)S(1)} collective-permute-done((f32[3,256,1]{2,1,0:T(8,128)S(1)}, f32[3,256,1]{2,1,0:T(8,128)S(1)}, u32[]{:S(2)}, u32[]{:S(2)}) %collective-permute-start) | collective-permute-done | bytes 3104 | tf_op jit(solution)/shard_map/ppermute | solution.py:15
  18.6 1.8 fusion.17
  20.4 1.1 fusion.1
  21.5 3.9 %collective-permute-start.3 = (f32[2,1,1024]{2,1,0:T(1,128)S(1)}, f32[2,1,1024]{2,1,0:T(1,128)S(1)}, u32[]{:S(2)}, u32[]{:S(2)}) collective-permute-start(f32[2,1,1024]{2,1,0:T(1,128)S(1)} %slice.280), channel_id=1, source_target_pairs={{0,16},{16,32},{32,48},{48,64},{64,80},{80,96},{96,112},{1,17},{17... | collective-permute-start | bytes 24584 | tf_op jit(solution)/shard_map/ppermute | solution.py:15
  25.6 2.7 collective-permute-start.2
  28.3 8.5 %collective-permute-done.2 = f32[2,256,1]{2,1,0:T(8,128)S(1)} collective-permute-done((f32[2,256,1]{2,1,0:T(8,128)S(1)}, f32[2,256,1]{2,1,0:T(8,128)S(1)}, u32[]{:S(2)}, u32[]{:S(2)}) %collective-permute-start.2) | collective-permute-done | bytes 2080 | tf_op jit(solution)/shard_map/ppermute | solution.py:15
  36.8 0.5 fusion.40
  37.4 1.9 collective-permute-start.5
  39.3 3.6 collective-permute-start.4
  43.1 0.3 slice.282
  43.5 2.1 collective-permute-done.4
  45.5 0.3 maximum_subtract_fusion.1
  45.9 1.3 fusion.3
  47.2 5.3 %collective-permute-start.7 = (f32[2,1,1024]{2,1,0:T(1,128)S(1)}, f32[2,1,1024]{2,1,0:T(1,128)S(1)}, u32[]{:S(2)}, u32[]{:S(2)}) collective-permute-start(f32[2,1,1024]{2,1,0:T(1,128)S(1)} %slice.290), channel_id=1, source_target_pairs={{0,16},{16,32},{32,48},{48,64},{64,80},{80,96},{96,112},{1,17},{17... | collective-permute-start | bytes 24584 | tf_op jit(solution)/shard_map/ppermute | solution.py:15
  52.6 1.9 collective-permute-start.6
  54.5 7.9 %collective-permute-done.6 = f32[2,256,1]{2,1,0:T(8,128)S(1)} collective-permute-done((f32[2,256,1]{2,1,0:T(8,128)S(1)}, f32[2,256,1]{2,1,0:T(8,128)S(1)}, u32[]{:S(2)}, u32[]{:S(2)}) %collective-permute-start.6) | collective-permute-done | bytes 2080 | tf_op jit(solution)/shard_map/ppermute | solution.py:15
  62.4 0.6 fusion.38
  63.0 1.9 collective-permute-start.9
  65.0 3.6 collective-permute-start.8
  68.7 0.3 slice.292
  69.1 1.6 collective-permute-done.8
  70.7 0.3 maximum_subtract_fusion.3
  71.1 3.2 multiply_reduce_fusion.6
  74.3 1.3 pad_maximum_fusion.17
  75.6 69.7 %psum.21 = f32[2]{0:T(128)S(1)} all-reduce(f32[2]{0:T(128)S(1)} %pad_maximum_fusion.17), channel_id=1, replica_groups=mesh['lat'=8,'lon'=16] {'lat','lon'}, use_global_device_ids=true, to_apply=%region_2.0 | all-reduce | flops 2 | bytes 16 | tf_op jit(solution)/shard_map/psum | solution.py:51
  145.4 0.6 fusion.52
  147.3 5.1 %multiply_subtract_fusion.1 = f32[2,256,1024]{2,1,0:T(8,128)S(1)} fusion(f32[2,256,1024]{2,1,0:T(8,128)} %get-tuple-element.15, f32[]{:T(128)S(6)} %div.23, f32[1,256,1024]{2,1,0:T(8,128)} %copy-done.19, f32[1,256,1024]{2,1,0:T(8,128)} %copy-done.18, f32[1,256,1024]{2,1,0:T(8,128)} %copy-done.1, f32[1,256,1024]{2,1,0:T(8,128)} %copy-done.4, ...), kind=kLoop, calls=%fused_computation.35 | loop fusion | flops 10485760 | bytes 14680068 | tf_op jit(solution)/shard_map/sub | solution.py:74
  152.4 2.3 collective-permute-start.11
  154.8 2.2 collective-permute-start.10
  157.0 9.5 %collective-permute-done.10 = f32[2,256,1]{2,1,0:T(8,128)S(1)} collective-permute-done((f32[2,256,1]{2,1,0:T(8,128)S(1)}, f32[2,256,1]{2,1,0:T(8,128)S(1)}, u32[]{:S(2)}, u32[]{:S(2)}) %collective-permute-start.10) | collective-permute-done | bytes 2080 | tf_op jit(solution)/shard_map/ppermute | solution.py:15
  166.5 0.5 fusion.36
  167.1 2.9 collective-permute-start.13
  170.0 1.9 collective-permute-start.12
  172.0 0.3 slice.302
  172.4 4.7 %collective-permute-done.12 = f32[1,256,1]{2,1,0:T(8,128)S(1)} collective-permute-done((f32[1,256,1]{2,1,0:T(8,128)S(1)}, f32[1,256,1]{2,1,0:T(8,128)S(1)}, u32[]{:S(2)}, u32[]{:S(2)}) %collective-permute-start.12) | collective-permute-done | bytes 1056 | tf_op jit(solution)/shard_map/ppermute | solution.py:15
  177.1 0.4 maximum_subtract_fusion.5
  177.6 2.9 multiply_reduce_fusion.4
  180.5 2.0 pad_maximum_fusion.18
  182.5 63.0 %psum.22 = f32[3]{0:T(128)S(1)} all-reduce(f32[3]{0:T(128)S(1)} %pad_maximum_fusion.18), channel_id=1, replica_groups=mesh['lat'=8,'lon'=16] {'lat','lon'}, use_global_device_ids=true, to_apply=%region_6.0 | all-reduce | flops 3 | bytes 24 | tf_op jit(solution)/shard_map/psum | solution.py:51
  245.5 0.7 fusion.51
  250.1 2.9 multiply_subtract_fusion
  253.1 2.0 collective-permute-start.15
  255.2 2.5 collective-permute-start.14
  257.7 9.0 %collective-permute-done.14 = f32[2,256,1]{2,1,0:T(8,128)S(1)} collective-permute-done((f32[2,256,1]{2,1,0:T(8,128)S(1)}, f32[2,256,1]{2,1,0:T(8,128)S(1)}, u32[]{:S(2)}, u32[]{:S(2)}) %collective-permute-start.14) | collective-permute-done | bytes 2080 | tf_op jit(solution)/shard_map/ppermute | solution.py:15
  266.7 0.5 fusion.34
  267.2 3.2 collective-permute-start.17
  270.4 2.0 collective-permute-start.16
  272.6 0.3 slice.312
  273.0 4.5 %collective-permute-done.16 = f32[1,256,1]{2,1,0:T(8,128)S(1)} collective-permute-done((f32[1,256,1]{2,1,0:T(8,128)S(1)}, f32[1,256,1]{2,1,0:T(8,128)S(1)}, u32[]{:S(2)}, u32[]{:S(2)}) %collective-permute-start.16) | collective-permute-done | bytes 1056 | tf_op jit(solution)/shard_map/ppermute | solution.py:15
  277.5 0.3 maximum_subtract_fusion.7
  277.9 2.2 multiply_reduce_fusion.1
  280.1 1.9 pad_maximum_fusion.19
  282.1 63.4 %psum.23 = f32[3]{0:T(128)S(1)} all-reduce(f32[3]{0:T(128)S(1)} %pad_maximum_fusion.19), channel_id=1, replica_groups=mesh['lat'=8,'lon'=16] {'lat','lon'}, use_global_device_ids=true, to_apply=%region_10.0 | all-reduce | flops 3 | bytes 24 | tf_op jit(solution)/shard_map/psum | solution.py:51
  345.4 0.6 fusion.50
  349.3 5.3 %multiply_add_fusion = f32[2,256,1024]{2,1,0:T(8,128)S(1)} fusion(f32[2,256,1024]{2,1,0:T(8,128)} %copy-done, f32[2,256,1024]{2,1,0:T(8,128)S(1)} %multiply_subtract_fusion.1, f32[]{:T(128)S(6)} %div.26, f32[]{:T(128)S(6)} %div.27, f32[]{:T(128)S(6)} %div.24, f32[]{:T(128)S(6)} %div.25, f32[]{:T(128)S(6)} %div.23, f32[1,256,1024]{2,1,0:T(8,128)} %copy-done.19, ...), kind=kLoop, calls=%fused_computation.27 | loop fusion | flops 14680064 | bytes 16777236 | tf_op jit(solution)/shard_map/add | solution.py:71
  354.6 2.9 collective-permute-start.19
  357.7 1.9 collective-permute-start.18
  359.6 10.4 %collective-permute-done.18 = f32[2,256,1]{2,1,0:T(8,128)S(1)} collective-permute-done((f32[2,256,1]{2,1,0:T(8,128)S(1)}, f32[2,256,1]{2,1,0:T(8,128)S(1)}, u32[]{:S(2)}, u32[]{:S(2)}) %collective-permute-start.18) | collective-permute-done | bytes 2080 | tf_op jit(solution)/shard_map/ppermute | solution.py:15
  370.0 2.1 fusion.30
  (81 shorter events, 2.1 us)
Async XLA Ops:
  0.6 1.5 copy-start.14
  0.6 1.8 copy-start.21
  2.5 16.1 %collective-permute-start.1 = (f32[3,1,1024]{2,1,0:T(1,128)S(1)}, f32[3,1,1024]{2,1,0:T(1,128)S(1)}, u32[]{:S(2)}, u32[]{:S(2)}) collective-permute-start(f32[3,1,1024]{2,1,0:T(1,128)S(1)} %pad_maximum_fusion.16), channel_id=1, source_target_pairs={{16,0},{32,16},{48,32},{64,48},{80,64},{96,80},{112,96},{17,1},{33... | collective-permute-start | bytes 36872 | tf_op jit(solution)/shard_map/ppermute | solution.py:15
  5.1 13.4 %collective-permute-start = (f32[3,256,1]{2,1,0:T(8,128)S(1)}, f32[3,256,1]{2,1,0:T(8,128)S(1)}, u32[]{:S(2)}, u32[]{:S(2)}) collective-permute-start(f32[3,256,1]{2,1,0:T(8,128)S(1)} %pad_maximum_fusion.15), channel_id=1, source_target_pairs={{1,0},{2,1},{3,2},{4,3},{5,4},{6,5},{7,6},{8,7},{9,8},{10,9},{11,1... | collective-permute-start | bytes 9224 | tf_op jit(solution)/shard_map/ppermute | solution.py:15
  10.4 8.2 %copy-start.22 = (s32[256,1024]{1,0:T(8,128)S(1)}, s32[256,1024]{1,0:T(8,128)}, u32[]{:S(2)}) copy-start(s32[256,1024]{1,0:T(8,128)} %param.7) | copy-start | bytes 3145732
  11.3 9.2 %copy-start.16 = (f32[256,1024]{1,0:T(8,128)S(1)}, f32[256,1024]{1,0:T(8,128)}, u32[]{:S(2)}) copy-start(f32[256,1024]{1,0:T(8,128)} %param.9) | copy-start | bytes 3145732
  11.3 9.2 %copy-start.17 = (f32[256,1024]{1,0:T(8,128)S(1)}, f32[256,1024]{1,0:T(8,128)}, u32[]{:S(2)}) copy-start(f32[256,1024]{1,0:T(8,128)} %param.8) | copy-start | bytes 3145732
  20.4 50.7 %copy-start.1 = (f32[1,256,1024]{2,1,0:T(8,128)}, f32[1,256,1024]{2,1,0:T(8,128)S(1)}, u32[]{:S(2)}) copy-start(f32[1,256,1024]{2,1,0:T(8,128)S(1)} %get-tuple-element.21) | copy-start | bytes 3145732
  20.4 50.7 %copy-start.4 = (f32[1,256,1024]{2,1,0:T(8,128)}, f32[1,256,1024]{2,1,0:T(8,128)S(1)}, u32[]{:S(2)}) copy-start(f32[1,256,1024]{2,1,0:T(8,128)S(1)} %get-tuple-element.22) | copy-start | bytes 3145732
  20.4 50.7 %copy-start.7 = (f32[1,256,1024]{2,1,0:T(8,128)}, f32[1,256,1024]{2,1,0:T(8,128)S(1)}, u32[]{:S(2)}) copy-start(f32[1,256,1024]{2,1,0:T(8,128)S(1)} %get-tuple-element.24) | copy-start | bytes 3145732
  20.4 50.7 %copy-start.12 = (f32[1,256,1024]{2,1,0:T(8,128)}, f32[1,256,1024]{2,1,0:T(8,128)S(1)}, u32[]{:S(2)}) copy-start(f32[1,256,1024]{2,1,0:T(8,128)S(1)} %get-tuple-element.20) | copy-start | bytes 3145732
  20.4 50.7 %copy-start.13 = (f32[1,256,1024]{2,1,0:T(8,128)}, f32[1,256,1024]{2,1,0:T(8,128)S(1)}, u32[]{:S(2)}) copy-start(f32[1,256,1024]{2,1,0:T(8,128)S(1)} %get-tuple-element.23) | copy-start | bytes 3145732
  21.5 15.3 %collective-permute-start.3 = (f32[2,1,1024]{2,1,0:T(1,128)S(1)}, f32[2,1,1024]{2,1,0:T(1,128)S(1)}, u32[]{:S(2)}, u32[]{:S(2)}) collective-permute-start(f32[2,1,1024]{2,1,0:T(1,128)S(1)} %slice.280), channel_id=1, source_target_pairs={{0,16},{16,32},{32,48},{48,64},{64,80},{80,96},{96,112},{1,17},{17... | collective-permute-start | bytes 24584 | tf_op jit(solution)/shard_map/ppermute | solution.py:15
  25.6 11.2 %collective-permute-start.2 = (f32[2,256,1]{2,1,0:T(8,128)S(1)}, f32[2,256,1]{2,1,0:T(8,128)S(1)}, u32[]{:S(2)}, u32[]{:S(2)}) collective-permute-start(f32[2,256,1]{2,1,0:T(8,128)S(1)} %slice.277), channel_id=1, source_target_pairs={{0,1},{1,2},{2,3},{3,4},{4,5},{5,6},{6,7},{7,8},{8,9},{9,10},{10,1... | collective-permute-start | bytes 6152 | tf_op jit(solution)/shard_map/ppermute | solution.py:15
  37.4 8.2 %collective-permute-start.5 = (f32[1,1,1024]{2,1,0:T(1,128)S(1)}, f32[1,1,1024]{2,1,0:T(1,128)S(1)}, u32[]{:S(2)}, u32[]{:S(2)}) collective-permute-start(f32[1,1,1024]{2,1,0:T(1,128)S(1)} %slice.285), channel_id=1, source_target_pairs={{16,0},{32,16},{48,32},{64,48},{80,64},{96,80},{112,96},{17,1},{33... | collective-permute-start | bytes 12296 | tf_op jit(solution)/shard_map/ppermute | solution.py:15
  39.3 6.2 %collective-permute-start.4 = (f32[1,256,1]{2,1,0:T(8,128)S(1)}, f32[1,256,1]{2,1,0:T(8,128)S(1)}, u32[]{:S(2)}, u32[]{:S(2)}) collective-permute-start(f32[1,256,1]{2,1,0:T(8,128)S(1)} %slice.283), channel_id=1, source_target_pairs={{1,0},{2,1},{3,2},{4,3},{5,4},{6,5},{7,6},{8,7},{9,8},{10,9},{11,1... | collective-permute-start | bytes 3080 | tf_op jit(solution)/shard_map/ppermute | solution.py:15
  45.9 25.2 %copy-start.18 = (f32[1,256,1024]{2,1,0:T(8,128)}, f32[1,256,1024]{2,1,0:T(8,128)S(1)}, u32[]{:S(2)}) copy-start(f32[1,256,1024]{2,1,0:T(8,128)S(1)} %get-tuple-element.31) | copy-start | bytes 3145732
  45.9 25.2 %copy-start.19 = (f32[1,256,1024]{2,1,0:T(8,128)}, f32[1,256,1024]{2,1,0:T(8,128)S(1)}, u32[]{:S(2)}) copy-start(f32[1,256,1024]{2,1,0:T(8,128)S(1)} %get-tuple-element.32) | copy-start | bytes 3145732
  47.2 15.2 %collective-permute-start.7 = (f32[2,1,1024]{2,1,0:T(1,128)S(1)}, f32[2,1,1024]{2,1,0:T(1,128)S(1)}, u32[]{:S(2)}, u32[]{:S(2)}) collective-permute-start(f32[2,1,1024]{2,1,0:T(1,128)S(1)} %slice.290), channel_id=1, source_target_pairs={{0,16},{16,32},{32,48},{48,64},{64,80},{80,96},{96,112},{1,17},{17... | collective-permute-start | bytes 24584 | tf_op jit(solution)/shard_map/ppermute | solution.py:15
  52.6 9.8 %collective-permute-start.6 = (f32[2,256,1]{2,1,0:T(8,128)S(1)}, f32[2,256,1]{2,1,0:T(8,128)S(1)}, u32[]{:S(2)}, u32[]{:S(2)}) collective-permute-start(f32[2,256,1]{2,1,0:T(8,128)S(1)} %slice.287), channel_id=1, source_target_pairs={{0,1},{1,2},{2,3},{3,4},{4,5},{5,6},{6,7},{7,8},{8,9},{9,10},{10,1... | collective-permute-start | bytes 6152 | tf_op jit(solution)/shard_map/ppermute | solution.py:15
  63.0 7.7 %collective-permute-start.9 = (f32[1,1,1024]{2,1,0:T(1,128)S(1)}, f32[1,1,1024]{2,1,0:T(1,128)S(1)}, u32[]{:S(2)}, u32[]{:S(2)}) collective-permute-start(f32[1,1,1024]{2,1,0:T(1,128)S(1)} %slice.295), channel_id=1, source_target_pairs={{16,0},{32,16},{48,32},{64,48},{80,64},{96,80},{112,96},{17,1},{33... | collective-permute-start | bytes 12296 | tf_op jit(solution)/shard_map/ppermute | solution.py:15
  65.0 5.7 %collective-permute-start.8 = (f32[1,256,1]{2,1,0:T(8,128)S(1)}, f32[1,256,1]{2,1,0:T(8,128)S(1)}, u32[]{:S(2)}, u32[]{:S(2)}) collective-permute-start(f32[1,256,1]{2,1,0:T(8,128)S(1)} %slice.293), channel_id=1, source_target_pairs={{1,0},{2,1},{3,2},{4,3},{5,4},{6,5},{7,6},{8,7},{9,8},{10,9},{11,1... | collective-permute-start | bytes 3080 | tf_op jit(solution)/shard_map/ppermute | solution.py:15
  152.4 14.1 %collective-permute-start.11 = (f32[2,1,1024]{2,1,0:T(1,128)S(1)}, f32[2,1,1024]{2,1,0:T(1,128)S(1)}, u32[]{:S(2)}, u32[]{:S(2)}) collective-permute-start(f32[2,1,1024]{2,1,0:T(1,128)S(1)} %slice.300), channel_id=1, source_target_pairs={{0,16},{16,32},{32,48},{48,64},{64,80},{80,96},{96,112},{1,17},{17... | collective-permute-start | bytes 24584 | tf_op jit(solution)/shard_map/ppermute | solution.py:15
  154.8 11.7 %collective-permute-start.10 = (f32[2,256,1]{2,1,0:T(8,128)S(1)}, f32[2,256,1]{2,1,0:T(8,128)S(1)}, u32[]{:S(2)}, u32[]{:S(2)}) collective-permute-start(f32[2,256,1]{2,1,0:T(8,128)S(1)} %slice.297), channel_id=1, source_target_pairs={{0,1},{1,2},{2,3},{3,4},{4,5},{5,6},{6,7},{7,8},{8,9},{9,10},{10,1... | collective-permute-start | bytes 6152 | tf_op jit(solution)/shard_map/ppermute | solution.py:15
  167.1 10.1 %collective-permute-start.13 = (f32[1,1,1024]{2,1,0:T(1,128)S(1)}, f32[1,1,1024]{2,1,0:T(1,128)S(1)}, u32[]{:S(2)}, u32[]{:S(2)}) collective-permute-start(f32[1,1,1024]{2,1,0:T(1,128)S(1)} %slice.305), channel_id=1, source_target_pairs={{16,0},{32,16},{48,32},{64,48},{80,64},{96,80},{112,96},{17,1},{33... | collective-permute-start | bytes 12296 | tf_op jit(solution)/shard_map/ppermute | solution.py:15
  170.0 7.1 %collective-permute-start.12 = (f32[1,256,1]{2,1,0:T(8,128)S(1)}, f32[1,256,1]{2,1,0:T(8,128)S(1)}, u32[]{:S(2)}, u32[]{:S(2)}) collective-permute-start(f32[1,256,1]{2,1,0:T(8,128)S(1)} %slice.303), channel_id=1, source_target_pairs={{1,0},{2,1},{3,2},{4,3},{5,4},{6,5},{7,6},{8,7},{9,8},{10,9},{11,1... | collective-permute-start | bytes 3080 | tf_op jit(solution)/shard_map/ppermute | solution.py:15
  172.4 5.1 %copy-start.2 = (f32[1,256,1024]{2,1,0:T(8,128)S(1)}, f32[1,256,1024]{2,1,0:T(8,128)}, u32[]{:S(2)}) copy-start(f32[1,256,1024]{2,1,0:T(8,128)} %copy-done.1) | copy-start | bytes 3145732
  172.4 5.1 %copy-start.5 = (f32[1,256,1024]{2,1,0:T(8,128)S(1)}, f32[1,256,1024]{2,1,0:T(8,128)}, u32[]{:S(2)}) copy-start(f32[1,256,1024]{2,1,0:T(8,128)} %copy-done.4) | copy-start | bytes 3145732
  172.4 5.1 %copy-start.8 = (f32[1,256,1024]{2,1,0:T(8,128)S(1)}, f32[1,256,1024]{2,1,0:T(8,128)}, u32[]{:S(2)}) copy-start(f32[1,256,1024]{2,1,0:T(8,128)} %copy-done.7) | copy-start | bytes 3145732
  172.4 5.1 %copy-start.10 = (f32[2,256,1024]{2,1,0:T(8,128)S(1)}, f32[2,256,1024]{2,1,0:T(8,128)}, u32[]{:S(2)}) copy-start(f32[2,256,1024]{2,1,0:T(8,128)} %get-tuple-element.15) | copy-start | bytes 6291460
  253.0 24.8 %copy-start = (f32[2,256,1024]{2,1,0:T(8,128)}, f32[2,256,1024]{2,1,0:T(8,128)S(1)}, u32[]{:S(2)}) copy-start(f32[2,256,1024]{2,1,0:T(8,128)S(1)} %multiply_subtract_fusion) | copy-start | bytes 6291460
  253.1 13.6 %collective-permute-start.15 = (f32[2,1,1024]{2,1,0:T(1,128)S(1)}, f32[2,1,1024]{2,1,0:T(1,128)S(1)}, u32[]{:S(2)}, u32[]{:S(2)}) collective-permute-start(f32[2,1,1024]{2,1,0:T(1,128)S(1)} %slice.310), channel_id=1, source_target_pairs={{0,16},{16,32},{32,48},{48,64},{64,80},{80,96},{96,112},{1,17},{17... | collective-permute-start | bytes 24584 | tf_op jit(solution)/shard_map/ppermute | solution.py:15
  255.2 11.4 %collective-permute-start.14 = (f32[2,256,1]{2,1,0:T(8,128)S(1)}, f32[2,256,1]{2,1,0:T(8,128)S(1)}, u32[]{:S(2)}, u32[]{:S(2)}) collective-permute-start(f32[2,256,1]{2,1,0:T(8,128)S(1)} %slice.307), channel_id=1, source_target_pairs={{0,1},{1,2},{2,3},{3,4},{4,5},{5,6},{6,7},{7,8},{8,9},{9,10},{10,1... | collective-permute-start | bytes 6152 | tf_op jit(solution)/shard_map/ppermute | solution.py:15
  267.2 10.3 %collective-permute-start.17 = (f32[1,1,1024]{2,1,0:T(1,128)S(1)}, f32[1,1,1024]{2,1,0:T(1,128)S(1)}, u32[]{:S(2)}, u32[]{:S(2)}) collective-permute-start(f32[1,1,1024]{2,1,0:T(1,128)S(1)} %slice.315), channel_id=1, source_target_pairs={{16,0},{32,16},{48,32},{64,48},{80,64},{96,80},{112,96},{17,1},{33... | collective-permute-start | bytes 12296 | tf_op jit(solution)/shard_map/ppermute | solution.py:15
  270.4 7.1 %collective-permute-start.16 = (f32[1,256,1]{2,1,0:T(8,128)S(1)}, f32[1,256,1]{2,1,0:T(8,128)S(1)}, u32[]{:S(2)}, u32[]{:S(2)}) collective-permute-start(f32[1,256,1]{2,1,0:T(8,128)S(1)} %slice.313), channel_id=1, source_target_pairs={{1,0},{2,1},{3,2},{4,3},{5,4},{6,5},{7,6},{8,7},{9,8},{10,9},{11,1... | collective-permute-start | bytes 3080 | tf_op jit(solution)/shard_map/ppermute | solution.py:15
  272.6 5.3 %copy-start.20 = (f32[2,256,1024]{2,1,0:T(8,128)S(1)}, f32[2,256,1024]{2,1,0:T(8,128)}, u32[]{:S(2)}) copy-start(f32[2,256,1024]{2,1,0:T(8,128)} %get-tuple-element.14) | copy-start | bytes 6291460
  273.0 4.9 %copy-start.3 = (f32[1,256,1024]{2,1,0:T(8,128)S(1)}, f32[1,256,1024]{2,1,0:T(8,128)}, u32[]{:S(2)}) copy-start(f32[1,256,1024]{2,1,0:T(8,128)} %copy-done.1) | copy-start | bytes 3145732
  273.0 4.9 %copy-start.6 = (f32[1,256,1024]{2,1,0:T(8,128)S(1)}, f32[1,256,1024]{2,1,0:T(8,128)}, u32[]{:S(2)}) copy-start(f32[1,256,1024]{2,1,0:T(8,128)} %copy-done.4) | copy-start | bytes 3145732
  273.0 4.9 %copy-start.9 = (f32[1,256,1024]{2,1,0:T(8,128)S(1)}, f32[1,256,1024]{2,1,0:T(8,128)}, u32[]{:S(2)}) copy-start(f32[1,256,1024]{2,1,0:T(8,128)} %copy-done.7) | copy-start | bytes 3145732
  273.0 4.9 %copy-start.11 = (f32[2,256,1024]{2,1,0:T(8,128)S(1)}, f32[2,256,1024]{2,1,0:T(8,128)}, u32[]{:S(2)}) copy-start(f32[2,256,1024]{2,1,0:T(8,128)} %get-tuple-element.15) | copy-start | bytes 6291460
  349.3 20.7 %copy-start.15 = (f32[256,1024]{1,0:T(8,128)S(1)}, f32[256,1024]{1,0:T(8,128)}, u32[]{:S(2)}) copy-start(f32[256,1024]{1,0:T(8,128)} %param.5) | copy-start | bytes 3145732
  354.6 15.3 %collective-permute-start.19 = (f32[2,1,1024]{2,1,0:T(1,128)S(1)}, f32[2,1,1024]{2,1,0:T(1,128)S(1)}, u32[]{:S(2)}, u32[]{:S(2)}) collective-permute-start(f32[2,1,1024]{2,1,0:T(1,128)S(1)} %slice.320), channel_id=1, source_target_pairs={{0,16},{16,32},{32,48},{48,64},{64,80},{80,96},{96,112},{1,17},{17... | collective-permute-start | bytes 24584 | tf_op jit(solution)/shard_map/ppermute | solution.py:15
  357.7 12.3 %collective-permute-start.18 = (f32[2,256,1]{2,1,0:T(8,128)S(1)}, f32[2,256,1]{2,1,0:T(8,128)S(1)}, u32[]{:S(2)}, u32[]{:S(2)}) collective-permute-start(f32[2,256,1]{2,1,0:T(8,128)S(1)} %slice.317), channel_id=1, source_target_pairs={{0,1},{1,2},{2,3},{3,4},{4,5},{5,6},{6,7},{7,8},{8,9},{9,10},{10,1... | collective-permute-start | bytes 6152 | tf_op jit(solution)/shard_map/ppermute | solution.py:15
where the time goes:
time: 373 us; the launch traced here: 372 us
  blocking collectives  196 us (53%)
  waiting for transfers between devices  65.5 us (18%)
  starting transfers between devices  55.9 us (15%)
  other arithmetic  38.4 us (10%)
  between operations  9.98 us (3%)
  local copies, waits for them, and re-layouts  6.32 us (2%)
    psum x3, blocking collectives, sums(): return lax.psum(local, ('lat', 'lon'))  196 us
    ppermute x20, waiting for transfers between devices, from_behind(): lax.ppermute(value, axis, [(source, source + steps) for source in range(l...  65.5 us
    ppermute x20, starting transfers between devices, from_behind(): lax.ppermute(value, axis, [(source, source + steps) for source in range(l...  55.9 us
    reduce_sum x3, other arithmetic, sums(): local = jnp.stack([jnp.sum(x * y) for x, y in pairs])  8.34 us
    sub x2, other arithmetic, per_device(): residual = residual - alpha * image  8 us
  transfers between devices with their start and end apart: 20, of which 10 were waited for; matrix products, arithmetic and copies ran while one was open for 1% of the time, Pallas kernels for 0%

commit v1 on v0

--- a/solution.py
+++ b/solution.py
@@ -48,7 +48,7 @@
 
 def sums(*pairs):
     local = jnp.stack([jnp.sum(x * y) for x, y in pairs])
-    return lax.psum(local, ("lat", "lon"))
+    return jnp.sum(lax.all_gather(local, ("lat", "lon")), axis=0)
 
 
 def per_device(surface, bathymetry, land_sea, flux_lon, flux_lat):

time: 373 us -> 372 us (level)
  waiting for transfers between devices: 65.5 us -> 58.2 us
  local copies, waits for them, and re-layouts: 6.32 us -> 11.7 us
    psum x3 -> x0, blocking collectives: 196 us -> none  [sums(): return lax.psum(local, ('lat', 'lon'))]
    unnamed x0 -> x3, blocking collectives: none -> 194 us
    ppermute x20, waiting for transfers between devices: 65.5 us -> 58.2 us  [from_behind(): lax.ppermute(value, axis, [(source, source + steps) for source in range(l...]
    unnamed x0 -> x3, other arithmetic: none -> 5.63 us
    another operation x3 -> x0, other arithmetic: 5.28 us -> none  [sums(): local = jnp.stack([jnp.sum(x * y) for x, y in pairs])]
  transfers between devices with their start and end apart: 20 -> 20, of which waited for: 10 -> 10; matrix products, arithmetic and copies ran while one was open for 1% -> 2% of each run, Pallas kernels for 0% -> 0%
where the time goes in v1:
time: 372 us; the launch traced here: 370 us
  blocking collectives  194 us (52%)
  waiting for transfers between devices  58.2 us (16%)
  starting transfers between devices  57.6 us (15%)
  other arithmetic  38.7 us (10%)
  local copies, waits for them, and re-layouts  11.7 us (3%)
  between operations  10.1 us (3%)
    unnamed x3, blocking collectives  194 us
    ppermute x20, waiting for transfers between devices, from_behind(): lax.ppermute(value, axis, [(source, source + steps) for source in range(l...  58.2 us
    ppermute x20, starting transfers between devices, from_behind(): lax.ppermute(value, axis, [(source, source + steps) for source in range(l...  57.6 us
    reduce_sum x3, other arithmetic, sums(): local = jnp.stack([jnp.sum(x * y) for x, y in pairs])  8.34 us
    sub x2, other arithmetic, per_device(): residual = residual - alpha * image  8 us
  transfers between devices with their start and end apart: 20, of which 10 were waited for; matrix products, arithmetic and copies ran while one was open for 2% of the time, Pallas kernels for 0%

profile of v1, /device:TPU:3, one launch (start us, length us, event | category | flops | bytes accessed | tf_op | source)
XLA Modules:
  0.0 370.3 jit_solution(3477920760447044872)
XLA Ops:
  0.7 1.5 convert_bitcast_fusion
  2.5 4.6 %collective-permute-start = (f32[3,256,1]{2,1,0:T(8,128)S(1)}, f32[3,256,1]{2,1,0:T(8,128)S(1)}, u32[]{:S(2)}, u32[]{:S(2)}) collective-permute-start(f32[3,256,1]{2,1,0:T(8,128)S(1)} %pad_maximum_fusion.15), channel_id=1, source_target_pairs={{1,0},{2,1},{3,2},{4,3},{5,4},{6,5},{7,6},{8,7},{9,8},{10,9},{11,1... | collective-permute-start | bytes 9224 | tf_op jit(solution)/shard_map/ppermute | solution.py:15
  7.2 2.9 collective-permute-start.1
  10.3 0.9 slice.266
  11.2 0.4 slice.269
  11.6 3.4 collective-permute-done
  15.0 1.5 fusion.17
  16.5 1.0 fusion.1
  17.6 5.0 %collective-permute-start.3 = (f32[2,1,1024]{2,1,0:T(1,128)S(1)}, f32[2,1,1024]{2,1,0:T(1,128)S(1)}, u32[]{:S(2)}, u32[]{:S(2)}) collective-permute-start(f32[2,1,1024]{2,1,0:T(1,128)S(1)} %slice.280), channel_id=1, source_target_pairs={{0,16},{16,32},{32,48},{48,64},{64,80},{80,96},{96,112},{1,17},{17... | collective-permute-start | bytes 24584 | tf_op jit(solution)/shard_map/ppermute | solution.py:15
  22.7 2.7 collective-permute-start.2
  25.4 8.1 %collective-permute-done.2 = f32[2,256,1]{2,1,0:T(8,128)S(1)} collective-permute-done((f32[2,256,1]{2,1,0:T(8,128)S(1)}, f32[2,256,1]{2,1,0:T(8,128)S(1)}, u32[]{:S(2)}, u32[]{:S(2)}) %collective-permute-start.2) | collective-permute-done | bytes 2080 | tf_op jit(solution)/shard_map/ppermute | solution.py:15
  33.5 0.6 fusion.40
  34.1 1.9 collective-permute-start.5
  36.0 3.6 collective-permute-start.4
  39.7 0.3 slice.282
  40.2 1.6 collective-permute-done.4
  41.8 0.5 maximum_subtract_fusion.1
  42.4 1.3 fusion.3
  43.7 6.1 %collective-permute-start.7 = (f32[2,1,1024]{2,1,0:T(1,128)S(1)}, f32[2,1,1024]{2,1,0:T(1,128)S(1)}, u32[]{:S(2)}, u32[]{:S(2)}) collective-permute-start(f32[2,1,1024]{2,1,0:T(1,128)S(1)} %slice.290), channel_id=1, source_target_pairs={{0,16},{16,32},{32,48},{48,64},{64,80},{80,96},{96,112},{1,17},{17... | collective-permute-start | bytes 24584 | tf_op jit(solution)/shard_map/ppermute | solution.py:15
  49.9 1.9 collective-permute-start.6
  51.8 7.6 %collective-permute-done.6 = f32[2,256,1]{2,1,0:T(8,128)S(1)} collective-permute-done((f32[2,256,1]{2,1,0:T(8,128)S(1)}, f32[2,256,1]{2,1,0:T(8,128)S(1)}, u32[]{:S(2)}, u32[]{:S(2)}) %collective-permute-start.6) | collective-permute-done | bytes 2080 | tf_op jit(solution)/shard_map/ppermute | solution.py:15
  59.4 0.6 fusion.38
  60.0 1.9 collective-permute-start.9
  62.0 3.4 collective-permute-start.8
  65.4 1.6 slice.292
  67.2 0.4 collective-permute-done.8
  67.7 0.3 maximum_subtract_fusion.3
  68.6 0.4 copy-done.8
  70.2 3.2 multiply_reduce_fusion.6
  73.4 1.4 maximum_dynamic-update-slice_fusion
  74.8 68.0 %all-reduce = f32[256]{0:T(256)S(1)} all-reduce(f32[256]{0:T(256)S(1)} %maximum_dynamic-update-slice_fusion), channel_id=2, replica_groups=mesh['lat'=8,'lon'=16] {'lat','lon'}, use_global_device_ids=true, to_apply=%add | all-reduce | flops 256 | bytes 2048
  143.0 0.6 fusion.52
  145.0 5.1 %multiply_subtract_fusion.1 = f32[2,256,1024]{2,1,0:T(8,128)S(1)} fusion(f32[2,256,1024]{2,1,0:T(8,128)} %get-tuple-element.15, f32[]{:T(128)S(6)} %div.23, f32[1,256,1024]{2,1,0:T(8,128)} %copy-done.25, f32[1,256,1024]{2,1,0:T(8,128)} %copy-done.23, f32[1,256,1024]{2,1,0:T(8,128)} %copy-done.1, f32[1,256,1024]{2,1,0:T(8,128)} %copy-done.4, ...), kind=kLoop, calls=%fused_computation.35 | loop fusion | flops 10485760 | bytes 14680068 | tf_op jit(solution)/shard_map/sub | solution.py:74
  150.1 2.3 collective-permute-start.11
  152.5 2.2 collective-permute-start.10
  154.7 9.5 %collective-permute-done.10 = f32[2,256,1]{2,1,0:T(8,128)S(1)} collective-permute-done((f32[2,256,1]{2,1,0:T(8,128)S(1)}, f32[2,256,1]{2,1,0:T(8,128)S(1)}, u32[]{:S(2)}, u32[]{:S(2)}) %collective-permute-start.10) | collective-permute-done | bytes 2080 | tf_op jit(solution)/shard_map/ppermute | solution.py:15
  164.2 0.5 fusion.36
  164.8 2.9 collective-permute-start.13
  167.7 1.9 collective-permute-start.12
  169.7 1.6 slice.302
  171.5 3.4 collective-permute-done.12
  174.8 0.4 maximum_subtract_fusion.5
  175.3 2.9 multiply_reduce_fusion.4
  178.2 2.1 maximum_dynamic-update-slice_fusion.1
  180.3 62.8 %all-reduce.1 = f32[384]{0:T(512)S(1)} all-reduce(f32[384]{0:T(512)S(1)} %maximum_dynamic-update-slice_fusion.1), channel_id=3, replica_groups=mesh['lat'=8,'lon'=16] {'lat','lon'}, use_global_device_ids=true, to_apply=%add.1 | all-reduce | flops 384 | bytes 3072
  243.3 0.7 fusion.51
  247.8 2.9 multiply_subtract_fusion
  250.8 2.2 collective-permute-start.15
  253.1 2.5 collective-permute-start.14
  255.6 9.2 %collective-permute-done.14 = f32[2,256,1]{2,1,0:T(8,128)S(1)} collective-permute-done((f32[2,256,1]{2,1,0:T(8,128)S(1)}, f32[2,256,1]{2,1,0:T(8,128)S(1)}, u32[]{:S(2)}, u32[]{:S(2)}) %collective-permute-start.14) | collective-permute-done | bytes 2080 | tf_op jit(solution)/shard_map/ppermute | solution.py:15
  264.8 0.5 fusion.34
  265.3 3.0 collective-permute-start.17
  268.3 1.9 collective-permute-start.16
  270.3 0.3 slice.312
  270.8 4.6 %collective-permute-done.16 = f32[1,256,1]{2,1,0:T(8,128)S(1)} collective-permute-done((f32[1,256,1]{2,1,0:T(8,128)S(1)}, f32[1,256,1]{2,1,0:T(8,128)S(1)}, u32[]{:S(2)}, u32[]{:S(2)}) %collective-permute-start.16) | collective-permute-done | bytes 1056 | tf_op jit(solution)/shard_map/ppermute | solution.py:15
  275.8 2.2 multiply_reduce_fusion.1
  278.0 2.1 maximum_dynamic-update-slice_fusion.2
  280.2 63.2 %all-reduce.2 = f32[384]{0:T(512)S(1)} all-reduce(f32[384]{0:T(512)S(1)} %maximum_dynamic-update-slice_fusion.2), channel_id=4, replica_groups=mesh['lat'=8,'lon'=16] {'lat','lon'}, use_global_device_ids=true, to_apply=%add.2 | all-reduce | flops 384 | bytes 3072
  343.7 0.7 fusion.50
  347.7 5.3 %multiply_add_fusion = f32[2,256,1024]{2,1,0:T(8,128)S(1)} fusion(f32[2,256,1024]{2,1,0:T(8,128)} %copy-done, f32[2,256,1024]{2,1,0:T(8,128)S(1)} %multiply_subtract_fusion.1, f32[]{:T(128)S(6)} %div.26, f32[]{:T(128)S(6)} %div.27, f32[]{:T(128)S(6)} %div.24, f32[]{:T(128)S(6)} %div.25, f32[]{:T(128)S(6)} %div.23, f32[1,256,1024]{2,1,0:T(8,128)} %copy-done.25, ...), kind=kLoop, calls=%fused_computation.27 | loop fusion | flops 14680064 | bytes 16777236 | tf_op jit(solution)/shard_map/add | solution.py:71
  353.0 2.8 collective-permute-start.19
  355.9 1.9 collective-permute-start.18
  357.9 10.3 %collective-permute-done.18 = f32[2,256,1]{2,1,0:T(8,128)S(1)} collective-permute-done((f32[2,256,1]{2,1,0:T(8,128)S(1)}, f32[2,256,1]{2,1,0:T(8,128)S(1)}, u32[]{:S(2)}, u32[]{:S(2)}) %collective-permute-start.18) | collective-permute-done | bytes 2080 | tf_op jit(solution)/shard_map/ppermute | solution.py:15
  368.2 2.1 fusion.30
  (112 shorter events, 4.9 us)
Async XLA Ops:
  0.6 1.5 copy-start.17
  0.6 1.8 copy-start.32
  2.5 12.4 %collective-permute-start = (f32[3,256,1]{2,1,0:T(8,128)S(1)}, f32[3,256,1]{2,1,0:T(8,128)S(1)}, u32[]{:S(2)}, u32[]{:S(2)}) collective-permute-start(f32[3,256,1]{2,1,0:T(8,128)S(1)} %pad_maximum_fusion.15), channel_id=1, source_target_pairs={{1,0},{2,1},{3,2},{4,3},{5,4},{6,5},{7,6},{8,7},{9,8},{10,9},{11,1... | collective-permute-start | bytes 9224 | tf_op jit(solution)/shard_map/ppermute | solution.py:15
  7.2 7.8 %collective-permute-start.1 = (f32[3,1,1024]{2,1,0:T(1,128)S(1)}, f32[3,1,1024]{2,1,0:T(1,128)S(1)}, u32[]{:S(2)}, u32[]{:S(2)}) collective-permute-start(f32[3,1,1024]{2,1,0:T(1,128)S(1)} %pad_maximum_fusion.16), channel_id=1, source_target_pairs={{16,0},{32,16},{48,32},{64,48},{80,64},{96,80},{112,96},{17,1},{33... | collective-permute-start | bytes 36872 | tf_op jit(solution)/shard_map/ppermute | solution.py:15
  11.2 3.8 %copy-start.33 = (s32[256,1024]{1,0:T(8,128)S(1)}, s32[256,1024]{1,0:T(8,128)}, u32[]{:S(2)}) copy-start(s32[256,1024]{1,0:T(8,128)} %param.7) | copy-start | bytes 3145732
  11.5 5.0 %copy-start.19 = (f32[256,1024]{1,0:T(8,128)S(1)}, f32[256,1024]{1,0:T(8,128)}, u32[]{:S(2)}) copy-start(f32[256,1024]{1,0:T(8,128)} %param.9) | copy-start | bytes 3145732
  11.6 5.0 %copy-start.21 = (f32[256,1024]{1,0:T(8,128)S(1)}, f32[256,1024]{1,0:T(8,128)}, u32[]{:S(2)}) copy-start(f32[256,1024]{1,0:T(8,128)} %param.8) | copy-start | bytes 3145732
  16.5 25.9 %copy-start.7 = (f32[1,256,1024]{2,1,0:T(8,128)}, f32[1,256,1024]{2,1,0:T(8,128)S(1)}, u32[]{:S(2)}) copy-start(f32[1,256,1024]{2,1,0:T(8,128)S(1)} %get-tuple-element.24) | copy-start | bytes 3145732
  16.5 25.9 %copy-start.13 = (f32[1,256,1024]{2,1,0:T(8,128)}, f32[1,256,1024]{2,1,0:T(8,128)S(1)}, u32[]{:S(2)}) copy-start(f32[1,256,1024]{2,1,0:T(8,128)S(1)} %get-tuple-element.20) | copy-start | bytes 3145732
  16.5 25.9 %copy-start.15 = (f32[1,256,1024]{2,1,0:T(8,128)}, f32[1,256,1024]{2,1,0:T(8,128)S(1)}, u32[]{:S(2)}) copy-start(f32[1,256,1024]{2,1,0:T(8,128)S(1)} %get-tuple-element.23) | copy-start | bytes 3145732
  16.5 51.5 %copy-start.1 = (f32[1,256,1024]{2,1,0:T(8,128)}, f32[1,256,1024]{2,1,0:T(8,128)S(1)}, u32[]{:S(2)}) copy-start(f32[1,256,1024]{2,1,0:T(8,128)S(1)} %get-tuple-element.21) | copy-start | bytes 3145732
  16.5 51.5 %copy-start.4 = (f32[1,256,1024]{2,1,0:T(8,128)}, f32[1,256,1024]{2,1,0:T(8,128)S(1)}, u32[]{:S(2)}) copy-start(f32[1,256,1024]{2,1,0:T(8,128)S(1)} %get-tuple-element.22) | copy-start | bytes 3145732
  17.6 15.9 %collective-permute-start.3 = (f32[2,1,1024]{2,1,0:T(1,128)S(1)}, f32[2,1,1024]{2,1,0:T(1,128)S(1)}, u32[]{:S(2)}, u32[]{:S(2)}) collective-permute-start(f32[2,1,1024]{2,1,0:T(1,128)S(1)} %slice.280), channel_id=1, source_target_pairs={{0,16},{16,32},{32,48},{48,64},{64,80},{80,96},{96,112},{1,17},{17... | collective-permute-start | bytes 24584 | tf_op jit(solution)/shard_map/ppermute | solution.py:15
  22.7 10.8 %collective-permute-start.2 = (f32[2,256,1]{2,1,0:T(8,128)S(1)}, f32[2,256,1]{2,1,0:T(8,128)S(1)}, u32[]{:S(2)}, u32[]{:S(2)}) collective-permute-start(f32[2,256,1]{2,1,0:T(8,128)S(1)} %slice.277), channel_id=1, source_target_pairs={{0,1},{1,2},{2,3},{3,4},{4,5},{5,6},{6,7},{7,8},{8,9},{9,10},{10,1... | collective-permute-start | bytes 6152 | tf_op jit(solution)/shard_map/ppermute | solution.py:15
  34.1 7.7 %collective-permute-start.5 = (f32[1,1,1024]{2,1,0:T(1,128)S(1)}, f32[1,1,1024]{2,1,0:T(1,128)S(1)}, u32[]{:S(2)}, u32[]{:S(2)}) collective-permute-start(f32[1,1,1024]{2,1,0:T(1,128)S(1)} %slice.285), channel_id=1, source_target_pairs={{16,0},{32,16},{48,32},{64,48},{80,64},{96,80},{112,96},{17,1},{33... | collective-permute-start | bytes 12296 | tf_op jit(solution)/shard_map/ppermute | solution.py:15
  36.0 5.8 %collective-permute-start.4 = (f32[1,256,1]{2,1,0:T(8,128)S(1)}, f32[1,256,1]{2,1,0:T(8,128)S(1)}, u32[]{:S(2)}, u32[]{:S(2)}) collective-permute-start(f32[1,256,1]{2,1,0:T(8,128)S(1)} %slice.283), channel_id=1, source_target_pairs={{1,0},{2,1},{3,2},{4,3},{5,4},{6,5},{7,6},{8,7},{9,8},{10,9},{11,1... | collective-permute-start | bytes 3080 | tf_op jit(solution)/shard_map/ppermute | solution.py:15
  42.3 1.3 copy-start.23
  42.3 1.3 copy-start.25
  43.7 15.7 %collective-permute-start.7 = (f32[2,1,1024]{2,1,0:T(1,128)S(1)}, f32[2,1,1024]{2,1,0:T(1,128)S(1)}, u32[]{:S(2)}, u32[]{:S(2)}) collective-permute-start(f32[2,1,1024]{2,1,0:T(1,128)S(1)} %slice.290), channel_id=1, source_target_pairs={{0,16},{16,32},{32,48},{48,64},{64,80},{80,96},{96,112},{1,17},{17... | collective-permute-start | bytes 24584 | tf_op jit(solution)/shard_map/ppermute | solution.py:15
  49.9 9.5 %collective-permute-start.6 = (f32[2,256,1]{2,1,0:T(8,128)S(1)}, f32[2,256,1]{2,1,0:T(8,128)S(1)}, u32[]{:S(2)}, u32[]{:S(2)}) collective-permute-start(f32[2,256,1]{2,1,0:T(8,128)S(1)} %slice.287), channel_id=1, source_target_pairs={{0,1},{1,2},{2,3},{3,4},{4,5},{5,6},{6,7},{7,8},{8,9},{9,10},{10,1... | collective-permute-start | bytes 6152 | tf_op jit(solution)/shard_map/ppermute | solution.py:15
  60.0 2.0 copy-start.28
  60.0 7.7 %collective-permute-start.9 = (f32[1,1,1024]{2,1,0:T(1,128)S(1)}, f32[1,1,1024]{2,1,0:T(1,128)S(1)}, u32[]{:S(2)}, u32[]{:S(2)}) collective-permute-start(f32[1,1,1024]{2,1,0:T(1,128)S(1)} %slice.295), channel_id=1, source_target_pairs={{16,0},{32,16},{48,32},{64,48},{80,64},{96,80},{112,96},{17,1},{33... | collective-permute-start | bytes 12296 | tf_op jit(solution)/shard_map/ppermute | solution.py:15
  62.0 5.7 %collective-permute-start.8 = (f32[1,256,1]{2,1,0:T(8,128)S(1)}, f32[1,256,1]{2,1,0:T(8,128)S(1)}, u32[]{:S(2)}, u32[]{:S(2)}) collective-permute-start(f32[1,256,1]{2,1,0:T(8,128)S(1)} %slice.293), channel_id=1, source_target_pairs={{1,0},{2,1},{3,2},{4,3},{5,4},{6,5},{7,6},{8,7},{9,8},{10,9},{11,1... | collective-permute-start | bytes 3080 | tf_op jit(solution)/shard_map/ppermute | solution.py:15
  65.4 1.7 copy-start.29
  67.0 1.2 copy-start.24
  67.0 1.5 copy-start.26
  67.2 1.7 copy-start.8
  67.2 2.0 copy-start.14
  67.2 2.3 copy-start.16
  67.2 2.7 copy-start.20
  67.2 2.9 copy-start.22
  150.1 14.1 %collective-permute-start.11 = (f32[2,1,1024]{2,1,0:T(1,128)S(1)}, f32[2,1,1024]{2,1,0:T(1,128)S(1)}, u32[]{:S(2)}, u32[]{:S(2)}) collective-permute-start(f32[2,1,1024]{2,1,0:T(1,128)S(1)} %slice.300), channel_id=1, source_target_pairs={{0,16},{16,32},{32,48},{48,64},{64,80},{80,96},{96,112},{1,17},{17... | collective-permute-start | bytes 24584 | tf_op jit(solution)/shard_map/ppermute | solution.py:15
  152.5 11.7 %collective-permute-start.10 = (f32[2,256,1]{2,1,0:T(8,128)S(1)}, f32[2,256,1]{2,1,0:T(8,128)S(1)}, u32[]{:S(2)}, u32[]{:S(2)}) collective-permute-start(f32[2,256,1]{2,1,0:T(8,128)S(1)} %slice.297), channel_id=1, source_target_pairs={{0,1},{1,2},{2,3},{3,4},{4,5},{5,6},{6,7},{7,8},{8,9},{9,10},{10,1... | collective-permute-start | bytes 6152 | tf_op jit(solution)/shard_map/ppermute | solution.py:15
  164.7 3.0 copy-start.30
  164.8 10.1 %collective-permute-start.13 = (f32[1,1,1024]{2,1,0:T(1,128)S(1)}, f32[1,1,1024]{2,1,0:T(1,128)S(1)}, u32[]{:S(2)}, u32[]{:S(2)}) collective-permute-start(f32[1,1,1024]{2,1,0:T(1,128)S(1)} %slice.305), channel_id=1, source_target_pairs={{16,0},{32,16},{48,32},{64,48},{80,64},{96,80},{112,96},{17,1},{33... | collective-permute-start | bytes 12296 | tf_op jit(solution)/shard_map/ppermute | solution.py:15
  167.7 7.1 %collective-permute-start.12 = (f32[1,256,1]{2,1,0:T(8,128)S(1)}, f32[1,256,1]{2,1,0:T(8,128)S(1)}, u32[]{:S(2)}, u32[]{:S(2)}) collective-permute-start(f32[1,256,1]{2,1,0:T(8,128)S(1)} %slice.303), channel_id=1, source_target_pairs={{1,0},{2,1},{3,2},{4,3},{5,4},{6,5},{7,6},{8,7},{9,8},{10,9},{11,1... | collective-permute-start | bytes 3080 | tf_op jit(solution)/shard_map/ppermute | solution.py:15
  169.6 1.7 copy-start.31
  171.4 3.8 %copy-start.2 = (f32[1,256,1024]{2,1,0:T(8,128)S(1)}, f32[1,256,1024]{2,1,0:T(8,128)}, u32[]{:S(2)}) copy-start(f32[1,256,1024]{2,1,0:T(8,128)} %copy-done.1) | copy-start | bytes 3145732
  171.4 3.8 %copy-start.5 = (f32[1,256,1024]{2,1,0:T(8,128)S(1)}, f32[1,256,1024]{2,1,0:T(8,128)}, u32[]{:S(2)}) copy-start(f32[1,256,1024]{2,1,0:T(8,128)} %copy-done.4) | copy-start | bytes 3145732
  171.4 3.8 %copy-start.9 = (f32[1,256,1024]{2,1,0:T(8,128)S(1)}, f32[1,256,1024]{2,1,0:T(8,128)}, u32[]{:S(2)}) copy-start(f32[1,256,1024]{2,1,0:T(8,128)} %copy-done.7) | copy-start | bytes 3145732
  171.4 3.8 %copy-start.11 = (f32[2,256,1024]{2,1,0:T(8,128)S(1)}, f32[2,256,1024]{2,1,0:T(8,128)}, u32[]{:S(2)}) copy-start(f32[2,256,1024]{2,1,0:T(8,128)} %get-tuple-element.15) | copy-start | bytes 6291460
  250.8 25.0 %copy-start = (f32[2,256,1024]{2,1,0:T(8,128)}, f32[2,256,1024]{2,1,0:T(8,128)S(1)}, u32[]{:S(2)}) copy-start(f32[2,256,1024]{2,1,0:T(8,128)S(1)} %multiply_subtract_fusion) | copy-start | bytes 6291460
  250.8 14.0 %collective-permute-start.15 = (f32[2,1,1024]{2,1,0:T(1,128)S(1)}, f32[2,1,1024]{2,1,0:T(1,128)S(1)}, u32[]{:S(2)}, u32[]{:S(2)}) collective-permute-start(f32[2,1,1024]{2,1,0:T(1,128)S(1)} %slice.310), channel_id=1, source_target_pairs={{0,16},{16,32},{32,48},{48,64},{64,80},{80,96},{96,112},{1,17},{17... | collective-permute-start | bytes 24584 | tf_op jit(solution)/shard_map/ppermute | solution.py:15
  253.1 11.6 %collective-permute-start.14 = (f32[2,256,1]{2,1,0:T(8,128)S(1)}, f32[2,256,1]{2,1,0:T(8,128)S(1)}, u32[]{:S(2)}, u32[]{:S(2)}) collective-permute-start(f32[2,256,1]{2,1,0:T(8,128)S(1)} %slice.307), channel_id=1, source_target_pairs={{0,1},{1,2},{2,3},{3,4},{4,5},{5,6},{6,7},{7,8},{8,9},{9,10},{10,1... | collective-permute-start | bytes 6152 | tf_op jit(solution)/shard_map/ppermute | solution.py:15
  265.3 10.1 %collective-permute-start.17 = (f32[1,1,1024]{2,1,0:T(1,128)S(1)}, f32[1,1,1024]{2,1,0:T(1,128)S(1)}, u32[]{:S(2)}, u32[]{:S(2)}) collective-permute-start(f32[1,1,1024]{2,1,0:T(1,128)S(1)} %slice.315), channel_id=1, source_target_pairs={{16,0},{32,16},{48,32},{64,48},{80,64},{96,80},{112,96},{17,1},{33... | collective-permute-start | bytes 12296 | tf_op jit(solution)/shard_map/ppermute | solution.py:15
  268.3 7.1 %collective-permute-start.16 = (f32[1,256,1]{2,1,0:T(8,128)S(1)}, f32[1,256,1]{2,1,0:T(8,128)S(1)}, u32[]{:S(2)}, u32[]{:S(2)}) collective-permute-start(f32[1,256,1]{2,1,0:T(8,128)S(1)} %slice.313), channel_id=1, source_target_pairs={{1,0},{2,1},{3,2},{4,3},{5,4},{6,5},{7,6},{8,7},{9,8},{10,9},{11,1... | collective-permute-start | bytes 3080 | tf_op jit(solution)/shard_map/ppermute | solution.py:15
  270.6 5.2 %copy-start.27 = (f32[2,256,1024]{2,1,0:T(8,128)S(1)}, f32[2,256,1024]{2,1,0:T(8,128)}, u32[]{:S(2)}) copy-start(f32[2,256,1024]{2,1,0:T(8,128)} %get-tuple-element.14) | copy-start | bytes 6291460
  270.8 5.0 %copy-start.3 = (f32[1,256,1024]{2,1,0:T(8,128)S(1)}, f32[1,256,1024]{2,1,0:T(8,128)}, u32[]{:S(2)}) copy-start(f32[1,256,1024]{2,1,0:T(8,128)} %copy-done.1) | copy-start | bytes 3145732
  270.8 5.0 %copy-start.6 = (f32[1,256,1024]{2,1,0:T(8,128)S(1)}, f32[1,256,1024]{2,1,0:T(8,128)}, u32[]{:S(2)}) copy-start(f32[1,256,1024]{2,1,0:T(8,128)} %copy-done.4) | copy-start | bytes 3145732
  270.8 5.0 %copy-start.10 = (f32[1,256,1024]{2,1,0:T(8,128)S(1)}, f32[1,256,1024]{2,1,0:T(8,128)}, u32[]{:S(2)}) copy-start(f32[1,256,1024]{2,1,0:T(8,128)} %copy-done.7) | copy-start | bytes 3145732
  270.8 5.0 %copy-start.12 = (f32[2,256,1024]{2,1,0:T(8,128)S(1)}, f32[2,256,1024]{2,1,0:T(8,128)}, u32[]{:S(2)}) copy-start(f32[2,256,1024]{2,1,0:T(8,128)} %get-tuple-element.15) | copy-start | bytes 6291460
  347.7 20.6 %copy-start.18 = (f32[256,1024]{1,0:T(8,128)S(1)}, f32[256,1024]{1,0:T(8,128)}, u32[]{:S(2)}) copy-start(f32[256,1024]{1,0:T(8,128)} %param.5) | copy-start | bytes 3145732
  353.0 15.2 %collective-permute-start.19 = (f32[2,1,1024]{2,1,0:T(1,128)S(1)}, f32[2,1,1024]{2,1,0:T(1,128)S(1)}, u32[]{:S(2)}, u32[]{:S(2)}) collective-permute-start(f32[2,1,1024]{2,1,0:T(1,128)S(1)} %slice.320), channel_id=1, source_target_pairs={{0,16},{16,32},{32,48},{48,64},{64,80},{80,96},{96,112},{1,17},{17... | collective-permute-start | bytes 24584 | tf_op jit(solution)/shard_map/ppermute | solution.py:15
  355.9 12.3 %collective-permute-start.18 = (f32[2,256,1]{2,1,0:T(8,128)S(1)}, f32[2,256,1]{2,1,0:T(8,128)S(1)}, u32[]{:S(2)}, u32[]{:S(2)}) collective-permute-start(f32[2,256,1]{2,1,0:T(8,128)S(1)} %slice.317), channel_id=1, source_target_pairs={{0,1},{1,2},{2,3},{3,4},{4,5},{5,6},{6,7},{7,8},{8,9},{9,10},{10,1... | collective-permute-start | bytes 6152 | tf_op jit(solution)/shard_map/ppermute | solution.py:15
